TPU v7x, 32 devices: a whole 2x2x4 slice. The times are simulated.
32 devices in a mesh: groups: 2 (over x), seq: 8 (over z, y), head: 2 (over core).
Axes of the slice: x: 2, y: 2, z: 4, core: 2. Of those that a mesh axis runs over, the one named last changes fastest.
Arguments:
- queries: bfloat16 [512, 4096], P(('groups', 'seq'), 'head'), parts along dimension 0, may hold values from -24 to 24
- vision: bfloat16 [4096, 7680], P(('groups', 'seq')), parts along dimension 0, may hold values from -6 to 6
- key_matrix: bfloat16 [7680, 512], P('seq', 'head'), may hold values from -0.0625 to 0.0625
- value_matrix: bfloat16 [7680, 512], P('seq', 'head'), may hold values from -0.0625 to 0.0625
- out_weight: bfloat16 [4096, 8192], P('head', 'seq'), may hold values from -0.09375 to 0.09375
- residual: bfloat16 [512, 8192], P(('groups', 'head'), 'seq'), parts along dimension 0, may hold values from -4 to 4
- query_norm_gain: float32 [128], replicated, may hold values from 1 to 12
- key_norm_gain: float32 [128], replicated, may hold values from 1 to 12
- attn_gate: float32 [1], replicated, may hold values from 0.5 to 2
Outputs:
- mixed: bfloat16 [512, 8192], P(('groups', 'head'), 'seq'), parts along dimension 0
There are 2 independent parts, one for each index of `groups`. A program takes and returns all parts, laid end to end along the dimension named above; an argument that names none is the same for every part. Nothing has to cross between parts.
All inputs are finite; a program needn't handle non-finite values.
Results may differ from a plain program's by a relative error of at most 0.015.
The roundings to bfloat16 on the way count: a program that leaves them out, or rounds other values in their place, can miss the bound.
Values may be sent and summed in bfloat16 or wider, within the bound.
A program may use at most 64 MiB of HBM per device.

v0:
```python
import jax
import jax.numpy as jnp
from jax import lax
from jax.sharding import PartitionSpec as P

HEAD_SIZE = 128


epsilon = 1e-05


def apply_norm(value_heads, gain):
    return (
        value_heads
        * lax.rsqrt(jnp.mean(value_heads * value_heads, axis=-1, keepdims=True) + epsilon)
        * gain
    )


def body(
    queries,
    vision,
    key_matrix,
    value_matrix,
    out_weight,
    residual,
    query_norm_gain,
    key_norm_gain,
    attn_gate,
):
    vision_rows = vision.shape[0]
    column_count = key_matrix.shape[1]
    expanded_keys = jnp.dot(
        vision,
        lax.all_gather(key_matrix, "seq", axis=0, tiled=True),
        preferred_element_type=jnp.float32,
    )
    expanded_values = jnp.dot(
        vision,
        lax.all_gather(value_matrix, "seq", axis=0, tiled=True),
        preferred_element_type=jnp.float32,
    )
    kv_local = column_count // HEAD_SIZE
    key_heads = apply_norm(
        expanded_keys.reshape(vision_rows, kv_local, HEAD_SIZE), key_norm_gain
    ).astype(jnp.bfloat16)
    value_heads = expanded_values.reshape(vision_rows, kv_local, HEAD_SIZE).astype(jnp.bfloat16)
    text_rows = queries.shape[0]
    heads_local = queries.shape[1] // HEAD_SIZE
    heads_per_group = heads_local // kv_local
    norm_result = apply_norm(
        queries.astype(jnp.float32).reshape(text_rows, kv_local, heads_per_group, HEAD_SIZE),
        query_norm_gain,
    ).astype(jnp.bfloat16)
    scale = HEAD_SIZE ** (-0.5)
    start_max = jnp.full((text_rows, kv_local, heads_per_group), -1e30, jnp.float32)
    start_den = jnp.zeros((text_rows, kv_local, heads_per_group), jnp.float32)
    start_num = jnp.zeros((text_rows, kv_local, heads_per_group, HEAD_SIZE), jnp.float32)
    key_piece = lax.all_gather(key_heads, "seq", axis=0, tiled=True)
    value_piece = lax.all_gather(value_heads, "seq", axis=0, tiled=True)
    piece_rows = key_piece.shape[0]
    rows_per_block = 512
    key_blocks = key_piece.reshape(
        piece_rows // rows_per_block, rows_per_block, kv_local, HEAD_SIZE
    )
    value_blocks = value_piece.reshape(
        piece_rows // rows_per_block, rows_per_block, kv_local, HEAD_SIZE
    )

    def advance(state_now, both):
        maxima, denominator, numerator = state_now
        scores = (
            jnp.einsum("tgqd,rgd->tgqr", norm_result, both[0], preferred_element_type=jnp.float32)
            * scale
        )
        new_max = jnp.maximum(maxima, jnp.max(scores, axis=-1))
        rescale = jnp.exp(maxima - new_max)
        weights = jnp.exp(scores - new_max[..., None])
        denominator = denominator * rescale + jnp.sum(weights, axis=-1)
        numerator = numerator * rescale[..., None] + jnp.einsum(
            "tgqr,rgd->tgqd",
            weights.astype(jnp.bfloat16),
            both[1],
            preferred_element_type=jnp.float32,
        )
        return ((new_max, denominator, numerator), None)

    maxima, denominator, numerator = lax.scan(
        advance, (start_max, start_den, start_num), (key_blocks, value_blocks)
    )[0]
    attended = (
        (numerator / denominator[..., None])
        .astype(jnp.bfloat16)
        .reshape(text_rows, heads_local * HEAD_SIZE)
    )
    partial_out = jnp.dot(
        lax.all_gather(attended, "seq", axis=0, tiled=True),
        out_weight,
        preferred_element_type=jnp.float32,
    )
    projected = lax.psum_scatter(
        partial_out.astype(jnp.bfloat16), "head", scatter_dimension=0, tiled=True
    ).astype(jnp.float32)
    return (residual.astype(jnp.float32) + jnp.tanh(attn_gate[0]) * projected).astype(jnp.bfloat16)


def solution(mesh):
    in_specs = (
        P(("groups", "seq"), "head"),
        P(("groups", "seq"), None),
        P("seq", "head"),
        P("seq", "head"),
        P("head", "seq"),
        P(("groups", "head"), "seq"),
        P(),
        P(),
        P(),
    )
    out_specs = P(("groups", "head"), "seq")
    return jax.shard_map(body, mesh=mesh, in_specs=in_specs, out_specs=out_specs, check_vma=False)
```

profile of v0, /device:TPU:1, one launch (start us, length us, event | category | flops | bytes accessed | tf_op | source)
XLA Modules:
  0.0 306.4 jit_solution(3217196021253669261)
XLA Ops:
  6.5 0.7 all-gather.6.cloned.1.call-update
  7.3 0.7 all-gather.10.cloned.1.call-update
  8.1 71.9 %all-gather.6.cloned.1.call-done = bf16[7680,256]{1,0:T(8,128)(2,1)} async-done(((bf16[960,256]{1,0:T(8,128)(2,1)}), bf16[7680,256]{1,0:T(8,128)(2,1)}) %all-gather.6.cloned.1.call-update) | async-done | bytes 3932176 | tf_op jit(solution)/shard_map/all_gather | solution.py:35
  80.0 5.0 %multiply_reduce_fusion.1 = (f32[256,2]{0,1:T(2,128)S(1)}, f32[256,256]{0,1:T(8,128)S(1)}) fusion(bf16[256,7680]{1,0:T(8,128)(2,1)} %param.12, bf16[7680,256]{1,0:T(8,128)(2,1)} %all-gather.6.cloned.1.call-done), kind=kOutput, calls=%fused_computation.27 | convolution fusion | flops 1006763520 | bytes 8128512 | tf_op jit(solution)/shard_map/dot_general | solution.py:33
  85.0 0.1 copy.23
  85.1 0.8 multiply_convert_fusion.1
  86.0 64.3 %all-gather.10.cloned.1.call-done = bf16[7680,256]{1,0:T(8,128)(2,1)} async-done(((bf16[960,256]{1,0:T(8,128)(2,1)}), bf16[7680,256]{1,0:T(8,128)(2,1)}) %all-gather.10.cloned.1.call-update) | async-done | bytes 3932176 | tf_op jit(solution)/shard_map/all_gather | solution.py:40
  150.3 4.9 %convolution_convert_fusion.1 = bf16[256,256]{0,1:T(8,128)(2,1)S(1)} fusion(bf16[256,7680]{1,0:T(8,128)(2,1)} %param.12, bf16[7680,256]{1,0:T(8,128)(2,1)} %all-gather.10.cloned.1.call-done), kind=kOutput, calls=%fused_computation.20 | convolution fusion | flops 1006698496 | bytes 7995392 | tf_op jit(solution)/shard_map/dot_general | solution.py:38
  155.3 0.7 copy.26
  156.2 0.2 multiply_reduce_fusion
  156.6 0.1 multiply_convert_fusion
  156.8 34.1 %all-gather.8.cloned.1.call-done = bf16[2048,2,128]{2,0,1:T(8,128)(2,1)} async-done(((bf16[256,2,128]{2,0,1:T(8,128)(2,1)}), bf16[2048,2,128]{2,0,1:T(8,128)(2,1)}) %all-gather.8.cloned.1.call-update) | async-done | bytes 1048592 | tf_op jit(solution)/shard_map/all_gather | solution.py:59
  190.9 41.0 %all-gather.12.cloned.1.call-done = bf16[2048,2,128]{2,0,1:T(8,128)(2,1)} async-done(((bf16[256,2,128]{2,0,1:T(8,128)(2,1)}), bf16[2048,2,128]{2,0,1:T(8,128)(2,1)}) %all-gather.12.cloned.1.call-update) | async-done | bytes 1048592 | tf_op jit(solution)/shard_map/all_gather | solution.py:60
  231.9 12.4 %while.15 = (s32[]{:T(128)}, f32[32,2,8]{0,2,1:T(8,128)S(1)}, f32[32,2,8]{0,2,1:T(8,128)S(1)}, f32[32,2,8,128]{3,0,2,1:T(8,128)S(1)}, bf16[4,512,2,128]{3,1,0,2:...) while((s32[]{:T(128)}, f32[32,2,8]{0,2,1:T(8,128)S(1)}, ...), condition=%wide.region_5.6_spmd.clone, body=%wide.region_2.5_spmd.clone.sunk | while | flops 135989760 | bytes 4358265 | solution.py:88
  231.9 1.3 fusion.31
  233.2 0.3 fusion.32
  233.6 1.4 fusion.34
  235.0 1.3 fusion.31
  236.3 0.3 fusion.32
  236.7 1.4 fusion.34
  238.1 1.3 fusion.31
  239.5 0.3 fusion.32
  239.8 1.4 fusion.34
  241.2 1.3 fusion.31
  242.6 0.3 fusion.32
  242.9 1.4 fusion.34
  244.3 0.1 divide_convert_fusion
  244.5 0.7 copy.38
  245.3 39.1 %all-gather.14.cloned.1.call-done = bf16[256,2048]{1,0:T(8,128)(2,1)} async-done(((bf16[32,2048]{1,0:T(8,128)(2,1)}), bf16[256,2048]{1,0:T(8,128)(2,1)}) %all-gather.14.cloned.1.call-update) | async-done | bytes 1048592 | tf_op jit(solution)/shard_map/all_gather | solution.py:97
  284.4 4.6 %convolution_convert_fusion = bf16[256,1024]{1,0:T(8,128)(2,1)} fusion(bf16[256,2048]{1,0:T(8,128)(2,1)} %all-gather.14.cloned.1.call-done, bf16[2048,1024]{1,0:T(8,128)(2,1)} %param.15), kind=kOutput, calls=%fused_computation.19 | convolution fusion | flops 1074003968 | bytes 5767168 | tf_op jit(solution)/shard_map/dot_general | solution.py:96
  289.7 8.1 %reduce-scatter.2.cloned.1.call-done = bf16[128,1024]{1,0:T(8,128)(2,1)} async-done(((bf16[256,1024]{1,0:T(8,128)(2,1)}), bf16[128,1024]{1,0:T(8,128)(2,1)}) %reduce-scatter.2.cloned.1.call-update) | async-done | bytes 262160 | tf_op jit(solution)/shard_map/reduce_scatter | solution.py:101
  297.8 1.7 add_convert_fusion
  (41 shorter events, 0.7 us)
Async XLA Ops:
  6.5 73.5 %all-gather.6.cloned.1.call-start = ((), (), s32[]{:S(2)}) async-start(), calls=%async_computation.1 | async-start | bytes 4423680 | tf_op jit(solution)/shard_map/all_gather | solution.py:35
  7.3 143.1 %all-gather.10.cloned.1.call-start = ((), (), s32[]{:S(2)}) async-start(), calls=%async_computation.3 | async-start | bytes 4423680 | tf_op jit(solution)/shard_map/all_gather | solution.py:40
  8.0 77.1 %copy-start.2 = (f32[128]{0:T(128)S(1)}, f32[128]{0:T(128)}, u32[]{:S(2)}) copy-start(f32[128]{0:T(128)} %param.18) | copy-start | bytes 1540
  8.0 182.8 %all-gather.8.cloned.1.call-start = ((), (), s32[]{:S(2)}) async-start(), calls=%async_computation.2 | async-start | bytes 1179648 | tf_op jit(solution)/shard_map/all_gather | solution.py:59
  85.9 70.2 %copy-start.1 = (bf16[32,2048]{1,0:T(8,128)(2,1)S(1)}, bf16[32,2048]{1,0:T(8,128)(2,1)}, u32[]{:S(2)}) copy-start(bf16[32,2048]{1,0:T(8,128)(2,1)} %param.11) | copy-start | bytes 393220
  85.9 70.6 %copy-start.3 = (f32[128]{0:T(128)S(1)}, f32[128]{0:T(128)}, u32[]{:S(2)}) copy-start(f32[128]{0:T(128)} %param.17) | copy-start | bytes 1540
  85.9 145.9 %all-gather.12.cloned.1.call-start = ((), (), s32[]{:S(2)}) async-start(), calls=%async_computation.4 | async-start | bytes 1179648 | tf_op jit(solution)/shard_map/all_gather | solution.py:60
  156.0 128.3 %all-gather.14.cloned.1.call-start = ((), (), s32[]{:S(2)}) async-start(), calls=%async_computation.5 | async-start | bytes 1179648 | tf_op jit(solution)/shard_map/all_gather | solution.py:97
  245.2 52.6 %copy-start = (bf16[128,1024]{1,0:T(8,128)(2,1)S(1)}, bf16[128,1024]{1,0:T(8,128)(2,1)}, u32[]{:S(2)}) copy-start(bf16[128,1024]{1,0:T(8,128)(2,1)} %param.16) | copy-start | bytes 786436
  245.3 52.6 %reduce-scatter.2.cloned.1.call-start = ((), (), s32[]{:S(2)}) async-start(), calls=%async_computation.6 | async-start | bytes 786432 | tf_op jit(solution)/shard_map/reduce_scatter | solution.py:101
Sparse Core Ops, SparseCore 0:
  9.5 70.4 all-gather.5
  82.2 68.1 all-gather.9
  152.5 38.2 all-gather.7
  192.9 38.9 all-gather.11
  245.4 38.9 all-gather.13
  289.1 8.6 reduce-scatter.1
where the time goes:
time: 307 us; the launch traced here: 306 us
  waiting for transfers between devices  260 us (85%)
  matrix products  25.4 us (8%)
  between operations  14.3 us (5%)
  other arithmetic  4.31 us (1%)
    all_gather x1, waiting for transfers between devices, body(): lax.all_gather(key_matrix, 'seq', axis=0, tiled=True)  71.9 us
    all_gather x1, waiting for transfers between devices, body(): lax.all_gather(value_matrix, 'seq', axis=0, tiled=True)  64.3 us
    all_gather x1, waiting for transfers between devices, body(): value_piece = lax.all_gather(value_heads, 'seq', axis=0, tiled=True)  41 us
    all_gather x1, waiting for transfers between devices, body(): lax.all_gather(attended, 'seq', axis=0, tiled=True)  39.1 us
    all_gather x1, waiting for transfers between devices, body(): key_piece = lax.all_gather(key_heads, 'seq', axis=0, tiled=True)  34.1 us
    reduce_scatter x1, waiting for transfers between devices, body(): lax.psum_scatter(partial_out.astype(jnp.bfloat16), 'head', scatter_dimens...  8.15 us
  transfers between devices with their start and end apart: 6, of which 6 were waited for; matrix products, arithmetic and copies ran while one was open for 4% of the time, Pallas kernels for 0%

commit v1 on v0

v1 whole, which is shorter than its diff:
```python
import functools

import jax
import jax.numpy as jnp
from jax import lax
from jax.experimental import pallas as pl
from jax.experimental.pallas import tpu as pltpu
from jax.sharding import PartitionSpec as P

HEAD_SIZE = 128
EPSILON = 1e-05
MESH = pl.DeviceIdType.MESH


def ring_columns(mesh):
    line = mesh.devices[0, :, 0]
    coords = [getattr(d, "coords", None) for d in line]
    if any(c is None for c in coords):
        return 1
    n = len(coords)

    def hops(order):
        return sum(
            sum(abs(a - b) for a, b in zip(coords[order[i]], coords[order[(i + 1) % n]]))
            for i in range(n)
        )

    straight = list(range(n))
    folded = straight[0::2] + straight[1::2][::-1]
    return 2 if hops(folded) < hops(straight) else 1


def norm(x, gain):
    return x * lax.rsqrt(jnp.mean(x * x, axis=-1, keepdims=True) + EPSILON) * gain


def kernel(
    n, folds, pairs,
    q_ref, vision_ref, key_ref, value_ref, out_w_ref, res_ref, qgain_ref, kgain_ref, gate_ref,
    out_ref,
    wk, wv, vis, ow, kbuf, vbuf, a0, a1, qs, pout, pin,
    load_sem, wsend, wrecv, xsend, xrecv, ksend, krecv, asend, arecv, psend, precv,
):
    group = lax.axis_index("groups")
    me = lax.axis_index("seq")
    head = lax.axis_index("head")
    half = n // folds

    def position(i):
        if folds == 1:
            return i
        z, y = i // 2, i % 2
        return z * (1 - y) + (n - 1 - z) * y

    def index(p):
        if folds == 1:
            return p
        y = p // half
        z = p * (1 - y) + (n - 1 - p) * y
        return z * 2 + y

    pos = position(me)

    def at(offset):
        return index(lax.rem(pos + (n + offset), n))

    neighbours = {1: at(1), -1: at(-1)}
    streams = [(1, 0, n // 2), (-1, 1, n // 2), (1, 1, n // 2 - 1), (-1, 0, n // 2 - 1)]

    def piece(view, send, recv, t, s, received):
        direction, b, _ = streams[t]
        owner = at(-direction * (s + received))
        v = view(b, owner)
        return pltpu.make_async_remote_copy(
            src_ref=v, dst_ref=v, send_sem=send.at[t, s], recv_sem=recv.at[t, s],
            device_id={"seq": neighbours[direction]}, device_id_type=MESH,
        )

    def begin(view, send, recv, b):
        for t, stream in enumerate(streams):
            if stream[1] == b and stream[2] > 0:
                piece(view, send, recv, t, 0, 0).start()

    def run(view, send, recv, arrived=None):
        for s in range(n // 2):
            for t, stream in enumerate(streams):
                if s < stream[2]:
                    piece(view, send, recv, t, s, 1).wait_recv()
                    if s + 1 < stream[2]:
                        piece(view, send, recv, t, s + 1, 0).start()
                    if arrived is not None:
                        arrived(t, s)

    def drain(view, send, recv):
        for t, stream in enumerate(streams):
            for s in range(stream[2]):
                piece(view, send, recv, t, s, 0).wait_send()

    rows = key_ref.shape[0]
    own = pl.ds(pl.multiple_of(me * rows, 16), rows)
    loads = [
        pltpu.make_async_copy(key_ref, wk.at[own], load_sem.at[0]),
        pltpu.make_async_copy(value_ref, wv.at[own], load_sem.at[1]),
        pltpu.make_async_copy(vision_ref, vis, load_sem.at[2]),
        pltpu.make_async_copy(out_w_ref, ow, load_sem.at[3]),
    ]
    for load in loads:
        load.start()

    barrier = pltpu.get_barrier_semaphore()
    for target in neighbours.values():
        pl.semaphore_signal(barrier, inc=1, device_id={"seq": target}, device_id_type=MESH)
    pl.semaphore_signal(barrier, inc=1, device_id={"head": 1 - head}, device_id_type=MESH)
    if pairs:
        odd = group % 2
        partner = group + 1 - 2 * odd
        pl.semaphore_signal(barrier, inc=1, device_id={"groups": partner}, device_id_type=MESH)
    pl.semaphore_wait(barrier, 4 if pairs else 3)

    loads[0].wait()
    loads[1].wait()

    shared = (rows * 3 // 10 + 15) // 16 * 16 if pairs else 0
    ringed = rows - shared
    weights = (wk, wv)

    def weight_view(b, owner):
        start = owner * rows
        if pairs:
            start = start + odd * shared
        return weights[b].at[pl.ds(pl.multiple_of(start, 16), ringed)]

    def cross(t, s, received):
        direction, b, _ = streams[t]
        owner = at(-direction * (s + 1))
        which = (1 - odd) if received else odd
        start = owner * rows + which * ringed
        v = weights[b].at[pl.ds(pl.multiple_of(start, 16), shared)]
        return pltpu.make_async_remote_copy(
            src_ref=v, dst_ref=v, send_sem=xsend.at[t, s], recv_sem=xrecv.at[t, s],
            device_id={"groups": partner}, device_id_type=MESH,
        )

    begin(weight_view, wsend, wrecv, 0)
    begin(weight_view, wsend, wrecv, 1)

    text = q_ref.shape[0]
    kv_local = key_ref.shape[1] // HEAD_SIZE
    heads_local = q_ref.shape[1] // HEAD_SIZE
    per_group = heads_local // kv_local
    for h in range(heads_local):
        x = q_ref[:, h * HEAD_SIZE:(h + 1) * HEAD_SIZE].astype(jnp.float32)
        qs[h * text:(h + 1) * text, :] = norm(x, qgain_ref[...]).astype(jnp.bfloat16)

    run(weight_view, wsend, wrecv, (lambda t, s: cross(t, s, False).start()) if pairs else None)
    if pairs:
        for t, stream in enumerate(streams):
            for s in range(stream[2]):
                cross(t, s, True).wait_recv()
    loads[2].wait()

    vrows, width = vis.shape
    mine = pl.ds(pl.multiple_of(me * vrows, 16), vrows)
    bufs = (kbuf, vbuf)

    def kv_view(b, owner):
        return bufs[b].at[pl.ds(pl.multiple_of(owner * vrows, 16), vrows)]

    keys = jnp.dot(vis[...], wk[...], preferred_element_type=jnp.float32)
    for g in range(kv_local):
        cols = slice(g * HEAD_SIZE, (g + 1) * HEAD_SIZE)
        kbuf[mine, cols] = norm(keys[:, cols], kgain_ref[...]).astype(jnp.bfloat16)
    begin(kv_view, ksend, krecv, 0)
    values = jnp.dot(vis[...], wv[...], preferred_element_type=jnp.float32)
    vbuf[mine, :] = values.astype(jnp.bfloat16)
    begin(kv_view, ksend, krecv, 1)
    run(kv_view, ksend, krecv)

    total = kbuf.shape[0]
    block = min(total, 2048)
    scale = HEAD_SIZE ** (-0.5)
    attended = (a0, a1)
    mine_text = pl.ds(pl.multiple_of(me * text, 16), text)

    def text_view(b, owner):
        return attended[b].at[pl.ds(pl.multiple_of(owner * text, 16), text)]

    groups_per_buffer = kv_local // 2
    for g in range(kv_local):
        cols = slice(g * HEAD_SIZE, (g + 1) * HEAD_SIZE)
        q = qs[g * per_group * text:(g + 1) * per_group * text, :]
        top = None
        for r in range(0, total, block):
            scores = lax.dot_general(
                q, kbuf[r:r + block, cols], (((1,), (1,)), ((), ())),
                preferred_element_type=jnp.float32,
            ) * scale
            high = jnp.max(scores, axis=-1, keepdims=True)
            new = high if top is None else jnp.maximum(top, high)
            weight = jnp.exp(scores - new)
            part = jnp.sum(weight, axis=-1, keepdims=True)
            product = jnp.dot(
                weight.astype(jnp.bfloat16), vbuf[r:r + block, cols],
                preferred_element_type=jnp.float32,
            )
            if top is None:
                den, num = part, product
            else:
                rescale = jnp.exp(top - new)
                den, num = den * rescale + part, num * rescale + product
            top = new
        result = (num / den).astype(jnp.bfloat16)
        b, inner = g // groups_per_buffer, g % groups_per_buffer
        for h in range(per_group):
            column = (inner * per_group + h) * HEAD_SIZE
            attended[b][mine_text, column:column + HEAD_SIZE] = result[h * text:(h + 1) * text, :]
        if inner == groups_per_buffer - 1:
            begin(text_view, asend, arecv, b)
    run(text_view, asend, arecv)
    loads[3].wait()

    out_rows = out_ref.shape[0]
    depth = a0.shape[1]

    def project(which):
        r = pl.ds(pl.multiple_of(which * out_rows, 16), out_rows)
        return jnp.dot(
            a0[r, :], ow[:depth, :], preferred_element_type=jnp.float32
        ) + jnp.dot(a1[r, :], ow[depth:, :], preferred_element_type=jnp.float32)

    pout[...] = project(1 - head).astype(jnp.bfloat16)
    swap = pltpu.make_async_remote_copy(
        src_ref=pout, dst_ref=pin, send_sem=psend, recv_sem=precv,
        device_id={"head": 1 - head}, device_id_type=MESH,
    )
    swap.start()
    projected = project(head)
    swap.wait_recv()
    out_ref[...] = (
        res_ref[...].astype(jnp.float32)
        + jnp.tanh(gate_ref[...]) * (projected + pin[...].astype(jnp.float32))
    ).astype(out_ref.dtype)

    swap.wait_send()
    drain(weight_view, wsend, wrecv)
    if pairs:
        for t, stream in enumerate(streams):
            for s in range(stream[2]):
                cross(t, s, False).wait_send()
    drain(kv_view, ksend, krecv)
    drain(text_view, asend, arecv)


def body(n, folds, pairs, queries, vision, key_matrix, value_matrix, out_weight, residual,
         query_norm_gain, key_norm_gain, attn_gate):
    rows, columns = key_matrix.shape
    vrows, width = vision.shape
    text, qcols = queries.shape
    bf16 = jnp.bfloat16
    vmem = pl.BlockSpec(memory_space=pltpu.VMEM)
    hbm = pl.BlockSpec(memory_space=pl.ANY)
    steps = pltpu.SemaphoreType.DMA((4, n // 2))
    return pl.pallas_call(
        functools.partial(kernel, n, folds, pairs),
        out_shape=jax.ShapeDtypeStruct(residual.shape, residual.dtype),
        in_specs=[vmem, hbm, hbm, hbm, hbm, vmem, vmem, vmem, vmem],
        out_specs=vmem,
        scratch_shapes=[
            pltpu.VMEM((n * rows, columns), bf16),
            pltpu.VMEM((n * rows, columns), bf16),
            pltpu.VMEM((vrows, width), bf16),
            pltpu.VMEM(out_weight.shape, bf16),
            pltpu.VMEM((n * vrows, columns), bf16),
            pltpu.VMEM((n * vrows, columns), bf16),
            pltpu.VMEM((n * text, qcols // 2), bf16),
            pltpu.VMEM((n * text, qcols // 2), bf16),
            pltpu.VMEM((text * qcols // HEAD_SIZE, HEAD_SIZE), bf16),
            pltpu.VMEM(residual.shape, bf16),
            pltpu.VMEM(residual.shape, bf16),
            pltpu.SemaphoreType.DMA((4,)),
            steps, steps, steps, steps, steps, steps, steps, steps,
            pltpu.SemaphoreType.DMA,
            pltpu.SemaphoreType.DMA,
        ],
        compiler_params=pltpu.CompilerParams(
            collective_id=0, has_side_effects=True, vmem_limit_bytes=60 * 1024 * 1024
        ),
    )(
        queries, vision, key_matrix, value_matrix, out_weight, residual,
        query_norm_gain.reshape(1, HEAD_SIZE), key_norm_gain.reshape(1, HEAD_SIZE),
        attn_gate.reshape(1, 1),
    )


def solution(mesh):
    in_specs = (
        P(("groups", "seq"), "head"),
        P(("groups", "seq"), None),
        P("seq", "head"),
        P("seq", "head"),
        P("head", "seq"),
        P(("groups", "head"), "seq"),
        P(),
        P(),
        P(),
    )
    out_specs = P(("groups", "head"), "seq")
    n = mesh.shape["seq"]
    pairs = mesh.shape["groups"] % 2 == 0
    local = functools.partial(body, n, ring_columns(mesh), pairs)
    return jax.shard_map(local, mesh=mesh, in_specs=in_specs, out_specs=out_specs, check_vma=False)
```

time: 307 us -> 113 us (0.37)
  waiting for transfers between devices: 260 us -> 0 us
  Pallas kernels: 0 us -> 111 us
  matrix products: 25.4 us -> 0 us
  between operations: 14.3 us -> 0.66 us
  other arithmetic: 4.31 us -> 0 us
    all_gather x5 -> x0, waiting for transfers between devices: 250 us -> none  [the longest x1 71.9 us: body(): lax.all_gather(key_matrix, 'seq', axis=0, tiled=True)]
    pallas_call x0 -> x1, Pallas kernels: none -> 111 us  [body(): pl.pallas_call(functools.partial(kernel, n, folds, pairs), out_shape=jax....]
    dot_general x11 -> x0, matrix products: 25.4 us -> none  [the longest x4 5.6 us: advance(): jnp.einsum('tgqr,rgd->tgqd', weights.astype(jnp.bfloat16), both[1], prefe...]
    reduce_scatter x1 -> x0, waiting for transfers between devices: 8.15 us -> none  [body(): lax.psum_scatter(partial_out.astype(jnp.bfloat16), 'head', scatter_dimens...]
  transfers between devices with their start and end apart: 6 -> 0, of which waited for: 6 -> 0; matrix products, arithmetic and copies ran while one was open for 4% -> 0% of each run, Pallas kernels for 0% -> 0%
where the time goes in v1:
time: 113 us
  Pallas kernels  111 us (98%)
  local copies, waits for them, and re-layouts  1.67 us (1%)
    pallas_call x1, Pallas kernels, body(): pl.pallas_call(functools.partial(kernel, n, folds, pairs), out_shape=jax....  111 us

profile of v1, /device:TPU:1, one launch (start us, length us, event | category | flops | bytes accessed | tf_op | source)
XLA Modules:
  0.0 113.0 jit_solution(13266332518221294877)
XLA Ops:
  0.7 110.7 %shard_map.91 = bf16[128,1024]{1,0:T(8,128)(2,1)} custom-call(bf16[32,2048]{1,0:T(8,128)(2,1)} %q_ref.1, bf16[256,7680]{1,0:T(8,128)(2,1)} %vision_ref.1, bf16[960,256]{1,0:T(8,128)(2,1)} %key_ref.1, bf16[960,256]{1,0:T(8,128)(2,1)} %value_ref.1, bf16[2048,1024]{1,0:T(8,128)(2,1)} %out_w_ref.1, bf16[128,1024]{1,0:T(8,128)(2,1)} %res_ref.1, ...), custom_call_target="tpu_custom_call" | custom-call | tf_op jit(solution)/shard_map/pallas_call | solution.py:263
  111.4 1.7 %copy.12 = bf16[128,1024]{1,0:T(8,128)(2,1)} copy(bf16[128,1024]{1,0:T(8,128)(2,1)} %shard_map.91) | data formatting | bytes 524288

commit v2 on v1

--- a/solution.py
+++ b/solution.py
@@ -27,7 +27,12 @@
 
     straight = list(range(n))
     folded = straight[0::2] + straight[1::2][::-1]
-    return 2 if hops(folded) < hops(straight) else 1
+    return 2 if n % 4 == 0 and hops(folded) < hops(straight) else 1
+
+
+def line_split(rows, pairs):
+    shared = rows * 9 // 20 // 16 * 16 if pairs else 0
+    return shared, rows - shared
 
 
 def norm(x, gain):
@@ -38,8 +43,9 @@
     n, folds, pairs,
     q_ref, vision_ref, key_ref, value_ref, out_w_ref, res_ref, qgain_ref, kgain_ref, gate_ref,
     out_ref,
-    wk, wv, vis, ow, kbuf, vbuf, a0, a1, qs, pout, pin,
+    wk, wv, vis, ow, kbuf, vbuf, a0, a1, qs, pout, pin, kown, kout, kin, vout, vin,
     load_sem, wsend, wrecv, xsend, xrecv, ksend, krecv, asend, arecv, psend, precv,
+    ysend, yrecv, csend, crecv,
 ):
     group = lax.axis_index("groups")
     me = lax.axis_index("seq")
@@ -97,83 +103,290 @@
                 piece(view, send, recv, t, s, 0).wait_send()
 
     rows = key_ref.shape[0]
-    own = pl.ds(pl.multiple_of(me * rows, 16), rows)
-    loads = [
-        pltpu.make_async_copy(key_ref, wk.at[own], load_sem.at[0]),
-        pltpu.make_async_copy(value_ref, wv.at[own], load_sem.at[1]),
-        pltpu.make_async_copy(vision_ref, vis, load_sem.at[2]),
-        pltpu.make_async_copy(out_w_ref, ow, load_sem.at[3]),
-    ]
-    for load in loads:
-        load.start()
-
-    barrier = pltpu.get_barrier_semaphore()
-    for target in neighbours.values():
-        pl.semaphore_signal(barrier, inc=1, device_id={"seq": target}, device_id_type=MESH)
-    pl.semaphore_signal(barrier, inc=1, device_id={"head": 1 - head}, device_id_type=MESH)
-    if pairs:
-        odd = group % 2
-        partner = group + 1 - 2 * odd
-        pl.semaphore_signal(barrier, inc=1, device_id={"groups": partner}, device_id_type=MESH)
-    pl.semaphore_wait(barrier, 4 if pairs else 3)
-
-    loads[0].wait()
-    loads[1].wait()
-
-    shared = (rows * 3 // 10 + 15) // 16 * 16 if pairs else 0
-    ringed = rows - shared
-    weights = (wk, wv)
-
-    def weight_view(b, owner):
-        start = owner * rows
-        if pairs:
-            start = start + odd * shared
-        return weights[b].at[pl.ds(pl.multiple_of(start, 16), ringed)]
-
-    def cross(t, s, received):
-        direction, b, _ = streams[t]
-        owner = at(-direction * (s + 1))
-        which = (1 - odd) if received else odd
-        start = owner * rows + which * ringed
-        v = weights[b].at[pl.ds(pl.multiple_of(start, 16), shared)]
-        return pltpu.make_async_remote_copy(
-            src_ref=v, dst_ref=v, send_sem=xsend.at[t, s], recv_sem=xrecv.at[t, s],
-            device_id={"groups": partner}, device_id_type=MESH,
-        )
-
-    begin(weight_view, wsend, wrecv, 0)
-    begin(weight_view, wsend, wrecv, 1)
-
+    vrows, width = vision_ref.shape
     text = q_ref.shape[0]
     kv_local = key_ref.shape[1] // HEAD_SIZE
     heads_local = q_ref.shape[1] // HEAD_SIZE
     per_group = heads_local // kv_local
-    for h in range(heads_local):
-        x = q_ref[:, h * HEAD_SIZE:(h + 1) * HEAD_SIZE].astype(jnp.float32)
-        qs[h * text:(h + 1) * text, :] = norm(x, qgain_ref[...]).astype(jnp.bfloat16)
-
-    run(weight_view, wsend, wrecv, (lambda t, s: cross(t, s, False).start()) if pairs else None)
-    if pairs:
-        for t, stream in enumerate(streams):
-            for s in range(stream[2]):
-                cross(t, s, True).wait_recv()
-    loads[2].wait()
-
-    vrows, width = vis.shape
+    odd = group % 2
+    partner = group + 1 - 2 * odd
+    weights = (wk, wv)
     mine = pl.ds(pl.multiple_of(me * vrows, 16), vrows)
     bufs = (kbuf, vbuf)
+    barrier = pltpu.get_barrier_semaphore()
+
+    def greet(**target):
+        pl.semaphore_signal(barrier, inc=1, device_id=target, device_id_type=MESH)
 
     def kv_view(b, owner):
         return bufs[b].at[pl.ds(pl.multiple_of(owner * vrows, 16), vrows)]
 
-    keys = jnp.dot(vis[...], wk[...], preferred_element_type=jnp.float32)
-    for g in range(kv_local):
-        cols = slice(g * HEAD_SIZE, (g + 1) * HEAD_SIZE)
-        kbuf[mine, cols] = norm(keys[:, cols], kgain_ref[...]).astype(jnp.bfloat16)
-    begin(kv_view, ksend, krecv, 0)
-    values = jnp.dot(vis[...], wv[...], preferred_element_type=jnp.float32)
-    vbuf[mine, :] = values.astype(jnp.bfloat16)
-    begin(kv_view, ksend, krecv, 1)
+    def queries():
+        for h in range(heads_local):
+            x = q_ref[:, h * HEAD_SIZE:(h + 1) * HEAD_SIZE].astype(jnp.float32)
+            qs[h * text:(h + 1) * text, :] = norm(x, qgain_ref[...]).astype(jnp.bfloat16)
+
+    def store_keys(keys):
+        for g in range(kv_local):
+            cols = slice(g * HEAD_SIZE, (g + 1) * HEAD_SIZE)
+            kbuf[mine, cols] = norm(keys[:, cols], kgain_ref[...]).astype(jnp.bfloat16)
+
+    def line_phase():
+        nz = half
+        z, y = me // 2, me % 2
+        other = z * 2 + 1 - y
+        padded = wk.shape[0] // nz
+        lead = y * (padded - rows)
+        shared, ringed = line_split(rows, pairs)
+        middle = ringed - shared
+
+        def slot(b, zz, start, size):
+            at_row = pl.multiple_of(zz * padded + lead + start, 16)
+            return weights[b].at[pl.ds(at_row, size)]
+
+        parts = [(odd * ringed, shared), (shared, middle)] if pairs else [(0, rows)]
+        loads = [
+            pltpu.make_async_copy(key_ref, slot(0, z, 0, rows), load_sem.at[0]),
+            pltpu.make_async_copy(value_ref, slot(1, z, 0, rows), load_sem.at[1]),
+            pltpu.make_async_copy(out_w_ref, ow, load_sem.at[3]),
+        ]
+        for zz in range(nz):
+            column = pl.multiple_of(zz * 2 * rows + y * (2 * rows - padded), HEAD_SIZE)
+            loads.append(pltpu.make_async_copy(
+                vision_ref.at[:, pl.ds(column, padded)],
+                vis.at[:vrows, zz * padded:(zz + 1) * padded], load_sem.at[4 + zz],
+            ))
+        for load in loads:
+            load.start()
+        greet(seq=other)
+        greet(head=1 - head)
+        if pairs:
+            greet(groups=partner)
+
+        @pl.when(z > 0)
+        def _():
+            greet(seq=(z - 1) * 2 + y)
+
+        @pl.when(z < nz - 1)
+        def _():
+            greet(seq=(z + 1) * 2 + y)
+
+        if padded > rows:
+            for zz in range(nz):
+                for w in weights:
+                    start = pl.multiple_of(zz * padded + (1 - y) * rows, 16)
+                    w[pl.ds(start, padded - rows), :] = jnp.zeros(
+                        (padded - rows, w.shape[1]), w.dtype)
+
+        peers = (3 if pairs else 2) + (z + nz - 1) // nz + (2 * nz - 2 - z) // nz
+        pl.semaphore_wait(barrier, peers)
+
+        def hop(b, d, s, part, zz):
+            start, size = parts[part]
+            v = slot(b, zz, start, size)
+            k = (b * 2 + (d + 1) // 2) * 2 + part
+            return pltpu.make_async_remote_copy(
+                src_ref=v, dst_ref=v, send_sem=wsend.at[k, s], recv_sem=wrecv.at[k, s],
+                device_id={"seq": (z + d) * 2 + y}, device_id_type=MESH,
+            )
+
+        def cross(b, d, s, zz, received):
+            which = (1 - odd) if received else odd
+            v = slot(b, zz, which * ringed, shared)
+            k = b * 2 + (d + 1) // 2
+            return pltpu.make_async_remote_copy(
+                src_ref=v, dst_ref=v, send_sem=xsend.at[k, s], recv_sem=xrecv.at[k, s],
+                device_id={"groups": partner}, device_id_type=MESH,
+            )
+
+        def can_send(d, s):
+            ahead = (z < nz - 1) if d == 1 else (z > 0)
+            behind = (z >= s) if d == 1 else (z + s <= nz - 1)
+            return jnp.logical_and(ahead, behind)
+
+        def gets(d, s):
+            return (z > s) if d == 1 else (z + s < nz - 1)
+
+        half_rows = vrows // 2
+
+        def vision_out(zz):
+            r = pl.ds(pl.multiple_of(head * half_rows, 16), half_rows)
+            column = pl.multiple_of(zz * 2 * rows + (1 - y) * (2 * rows - padded), HEAD_SIZE)
+            to = pl.ds(pl.multiple_of(vrows + head * half_rows, 16), half_rows)
+            return pltpu.make_async_remote_copy(
+                src_ref=vision_ref.at[r, pl.ds(column, padded)],
+                dst_ref=vis.at[to, zz * padded:(zz + 1) * padded],
+                send_sem=ysend.at[zz], recv_sem=yrecv.at[zz],
+                device_id={"seq": other}, device_id_type=MESH,
+            )
+
+        def vision_pass(zz, received):
+            which = (1 - head) if received else head
+            r = pl.ds(pl.multiple_of(vrows + which * half_rows, 16), half_rows)
+            v = vis.at[r, zz * padded:(zz + 1) * padded]
+            return pltpu.make_async_remote_copy(
+                src_ref=v, dst_ref=v, send_sem=csend.at[zz], recv_sem=crecv.at[zz],
+                device_id={"head": 1 - head}, device_id_type=MESH,
+            )
+
+        def begin_line(b):
+            loads[b].wait()
+            for d in (1, -1):
+                @pl.when(can_send(d, 0))
+                def _():
+                    for part in range(len(parts)):
+                        hop(b, d, 0, part, z).start()
+
+        def step(b, s):
+            for part in range(len(parts)):
+                for d in (1, -1):
+                    zz = z - d * (s + 1)
+
+                    @pl.when(gets(d, s))
+                    def _():
+                        hop(b, d, s, part, zz).wait_recv()
+                        if s + 1 < nz - 1:
+                            @pl.when(can_send(d, s + 1))
+                            def _():
+                                hop(b, d, s + 1, part, zz).start()
+                        if part == 0 and pairs:
+                            cross(b, d, s, zz, False).start()
+
+        def finish(b):
+            if pairs:
+                for s in range(nz - 1):
+                    for d in (1, -1):
+                        @pl.when(gets(d, s))
+                        def _():
+                            cross(b, d, s, z - d * (s + 1), True).wait_recv()
+
+        def give(b):
+            src, dst = ((kout, kin), (vout, vin))[b]
+            return pltpu.make_async_remote_copy(
+                src_ref=src, dst_ref=dst, send_sem=ysend.at[nz + b], recv_sem=yrecv.at[nz + b],
+                device_id={"seq": other}, device_id_type=MESH,
+            )
+
+        def product(b, first):
+            r = slice(0, vrows) if first else slice(vrows, 2 * vrows)
+            return jnp.dot(vis[r, :], weights[b][...], preferred_element_type=jnp.float32)
+
+        begin_line(0)
+        for zz in range(nz):
+            vision_out(zz).start()
+        queries()
+        for s in range(nz - 1):
+            step(0, s)
+        begin_line(1)
+        finish(0)
+        for s in range(nz - 1):
+            if s == nz - 2:
+                for load in loads[3:]:
+                    load.wait()
+                for zz in range(nz):
+                    vision_out(zz).wait_recv()
+                    vision_pass(zz, False).start()
+                for zz in range(nz):
+                    vision_pass(zz, True).wait_recv()
+                kout[...] = product(0, False)
+                give(0).start()
+                kown[...] = product(0, True)
+            step(1, s)
+        give(0).wait_recv()
+        store_keys(kown[...] + kin[...])
+        begin(kv_view, ksend, krecv, 0)
+        finish(1)
+        vout[...] = product(1, False).astype(vout.dtype)
+        give(1).start()
+        values = product(1, True)
+        give(1).wait_recv()
+        vbuf[mine, :] = (values + vin[...].astype(jnp.float32)).astype(jnp.bfloat16)
+        begin(kv_view, ksend, krecv, 1)
+
+        def settle():
+            for b in range(2):
+                give(b).wait_send()
+                for s in range(nz - 1):
+                    for d in (1, -1):
+                        @pl.when(can_send(d, s))
+                        def _():
+                            for part in range(len(parts)):
+                                hop(b, d, s, part, z - d * s).wait_send()
+
+                        if pairs:
+                            @pl.when(gets(d, s))
+                            def _():
+                                cross(b, d, s, z - d * (s + 1), False).wait_send()
+            for zz in range(nz):
+                vision_out(zz).wait_send()
+                vision_pass(zz, False).wait_send()
+
+        return loads[2], settle
+
+    def ring_phase():
+        own = pl.ds(pl.multiple_of(me * rows, 16), rows)
+        loads = [
+            pltpu.make_async_copy(key_ref, wk.at[own], load_sem.at[0]),
+            pltpu.make_async_copy(value_ref, wv.at[own], load_sem.at[1]),
+            pltpu.make_async_copy(vision_ref, vis, load_sem.at[2]),
+            pltpu.make_async_copy(out_w_ref, ow, load_sem.at[3]),
+        ]
+        for load in loads:
+            load.start()
+        for target in neighbours.values():
+            greet(seq=target)
+        greet(head=1 - head)
+        if pairs:
+            greet(groups=partner)
+        pl.semaphore_wait(barrier, 4 if pairs else 3)
+        loads[0].wait()
+        loads[1].wait()
+        shared = (rows * 3 // 10 + 15) // 16 * 16 if pairs else 0
+        ringed = rows - shared
+
+        def weight_view(b, owner):
+            start = owner * rows
+            if pairs:
+                start = start + odd * shared
+            return weights[b].at[pl.ds(pl.multiple_of(start, 16), ringed)]
+
+        def cross(t, s, received):
+            direction, b, _ = streams[t]
+            owner = at(-direction * (s + 1))
+            which = (1 - odd) if received else odd
+            start = owner * rows + which * ringed
+            v = weights[b].at[pl.ds(pl.multiple_of(start, 16), shared)]
+            return pltpu.make_async_remote_copy(
+                src_ref=v, dst_ref=v, send_sem=xsend.at[t, s], recv_sem=xrecv.at[t, s],
+                device_id={"groups": partner}, device_id_type=MESH,
+            )
+
+        begin(weight_view, wsend, wrecv, 0)
+        begin(weight_view, wsend, wrecv, 1)
+        queries()
+        run(weight_view, wsend, wrecv,
+            (lambda t, s: cross(t, s, False).start()) if pairs else None)
+        if pairs:
+            for t, stream in enumerate(streams):
+                for s in range(stream[2]):
+                    cross(t, s, True).wait_recv()
+        loads[2].wait()
+        store_keys(jnp.dot(vis[...], wk[...], preferred_element_type=jnp.float32))
+        begin(kv_view, ksend, krecv, 0)
+        values = jnp.dot(vis[...], wv[...], preferred_element_type=jnp.float32)
+        vbuf[mine, :] = values.astype(jnp.bfloat16)
+        begin(kv_view, ksend, krecv, 1)
+
+        def settle():
+            drain(weight_view, wsend, wrecv)
+            if pairs:
+                for t, stream in enumerate(streams):
+                    for s in range(stream[2]):
+                        cross(t, s, False).wait_send()
+
+        return loads[3], settle
+
+    out_load, settle = (line_phase if folds == 2 else ring_phase)()
     run(kv_view, ksend, krecv)
 
     total = kbuf.shape[0]
@@ -217,7 +430,7 @@
         if inner == groups_per_buffer - 1:
             begin(text_view, asend, arecv, b)
     run(text_view, asend, arecv)
-    loads[3].wait()
+    out_load.wait()
 
     out_rows = out_ref.shape[0]
     depth = a0.shape[1]
@@ -242,11 +455,7 @@
     ).astype(out_ref.dtype)
 
     swap.wait_send()
-    drain(weight_view, wsend, wrecv)
-    if pairs:
-        for t, stream in enumerate(streams):
-            for s in range(stream[2]):
-                cross(t, s, False).wait_send()
+    settle()
     drain(kv_view, ksend, krecv)
     drain(text_view, asend, arecv)
 
@@ -260,15 +469,24 @@
     vmem = pl.BlockSpec(memory_space=pltpu.VMEM)
     hbm = pl.BlockSpec(memory_space=pl.ANY)
     steps = pltpu.SemaphoreType.DMA((4, n // 2))
+    hops = pltpu.SemaphoreType.DMA((8, n // 2))
+    if folds == 2:
+        depth = n // 2 * (-(-rows // HEAD_SIZE) * HEAD_SIZE)
+        seen = (2 * vrows, depth)
+        part = (vrows, columns)
+    else:
+        depth = n * rows
+        seen = (vrows, width)
+        part = (16, HEAD_SIZE)
     return pl.pallas_call(
         functools.partial(kernel, n, folds, pairs),
         out_shape=jax.ShapeDtypeStruct(residual.shape, residual.dtype),
         in_specs=[vmem, hbm, hbm, hbm, hbm, vmem, vmem, vmem, vmem],
         out_specs=vmem,
         scratch_shapes=[
-            pltpu.VMEM((n * rows, columns), bf16),
-            pltpu.VMEM((n * rows, columns), bf16),
-            pltpu.VMEM((vrows, width), bf16),
+            pltpu.VMEM((depth, columns), bf16),
+            pltpu.VMEM((depth, columns), bf16),
+            pltpu.VMEM(seen, bf16),
             pltpu.VMEM(out_weight.shape, bf16),
             pltpu.VMEM((n * vrows, columns), bf16),
             pltpu.VMEM((n * vrows, columns), bf16),
@@ -277,10 +495,19 @@
             pltpu.VMEM((text * qcols // HEAD_SIZE, HEAD_SIZE), bf16),
             pltpu.VMEM(residual.shape, bf16),
             pltpu.VMEM(residual.shape, bf16),
-            pltpu.SemaphoreType.DMA((4,)),
-            steps, steps, steps, steps, steps, steps, steps, steps,
+            pltpu.VMEM(part, jnp.float32),
+            pltpu.VMEM(part, jnp.float32),
+            pltpu.VMEM(part, jnp.float32),
+            pltpu.VMEM(part, bf16),
+            pltpu.VMEM(part, bf16),
+            pltpu.SemaphoreType.DMA((4 + n // 2,)),
+            hops, hops, steps, steps, steps, steps, steps, steps,
             pltpu.SemaphoreType.DMA,
             pltpu.SemaphoreType.DMA,
+            pltpu.SemaphoreType.DMA((n // 2 + 2,)),
+            pltpu.SemaphoreType.DMA((n // 2 + 2,)),
+            pltpu.SemaphoreType.DMA((n // 2,)),
+            pltpu.SemaphoreType.DMA((n // 2,)),
         ],
         compiler_params=pltpu.CompilerParams(
             collective_id=0, has_side_effects=True, vmem_limit_bytes=60 * 1024 * 1024

time: 113 us -> 98.6 us (0.87)
  Pallas kernels: 111 us -> 96.1 us
    pallas_call x1, Pallas kernels: 111 us -> 96.1 us  [body(): pl.pallas_call(functools.partial(kernel, n, folds, pairs), out_shape=jax....]
where the time goes in v2:
time: 98.6 us; the launch traced here: 98.4 us
  Pallas kernels  96.1 us (97%)
  local copies, waits for them, and re-layouts  1.67 us (2%)
    pallas_call x1, Pallas kernels, body(): pl.pallas_call(functools.partial(kernel, n, folds, pairs), out_shape=jax....  96.1 us

profile of v2, /device:TPU:1, one launch (start us, length us, event | category | flops | bytes accessed | tf_op | source)
XLA Modules:
  0.0 98.4 jit_solution(16074994852182836778)
XLA Ops:
  0.7 96.1 %shard_map.91 = bf16[128,1024]{1,0:T(8,128)(2,1)} custom-call(bf16[32,2048]{1,0:T(8,128)(2,1)} %q_ref.1, bf16[256,7680]{1,0:T(8,128)(2,1)} %vision_ref.1, bf16[960,256]{1,0:T(8,128)(2,1)} %key_ref.1, bf16[960,256]{1,0:T(8,128)(2,1)} %value_ref.1, bf16[2048,1024]{1,0:T(8,128)(2,1)} %out_w_ref.1, bf16[128,1024]{1,0:T(8,128)(2,1)} %res_ref.1, ...), custom_call_target="tpu_custom_call" | custom-call | tf_op jit(solution)/shard_map/pallas_call | solution.py:481
  96.7 1.7 %copy.12 = bf16[128,1024]{1,0:T(8,128)(2,1)} copy(bf16[128,1024]{1,0:T(8,128)(2,1)} %shard_map.91) | data formatting | bytes 524288

commit v3 on v2

--- a/solution.py
+++ b/solution.py
@@ -31,7 +31,7 @@
 
 
 def line_split(rows, pairs):
-    shared = rows * 9 // 20 // 16 * 16 if pairs else 0
+    shared = rows * 19 // 40 // 16 * 16 if pairs else 0
     return shared, rows - shared
 
 
@@ -156,8 +156,8 @@
                 vision_ref.at[:, pl.ds(column, padded)],
                 vis.at[:vrows, zz * padded:(zz + 1) * padded], load_sem.at[4 + zz],
             ))
-        for load in loads:
-            load.start()
+        loads[0].start()
+        loads[1].start()
         greet(seq=other)
         greet(head=1 - head)
         if pairs:
@@ -274,6 +274,8 @@
         begin_line(0)
         for zz in range(nz):
             vision_out(zz).start()
+        for load in loads[2:]:
+            load.start()
         queries()
         for s in range(nz - 1):
             step(0, s)

time: 98.6 us -> 97.6 us (0.990)
  Pallas kernels: 96.1 us -> 95.1 us
where the time goes in v3:
time: 97.6 us; the launch traced here: 97.5 us
  Pallas kernels  95.1 us (97%)
  local copies, waits for them, and re-layouts  1.67 us (2%)
    pallas_call x1, Pallas kernels, body(): pl.pallas_call(functools.partial(kernel, n, folds, pairs), out_shape=jax....  95.1 us

profile of v3, /device:TPU:1, one launch (start us, length us, event | category | flops | bytes accessed | tf_op | source)
XLA Modules:
  0.0 97.5 jit_solution(662424898876436655)
XLA Ops:
  0.7 95.1 %shard_map.91 = bf16[128,1024]{1,0:T(8,128)(2,1)} custom-call(bf16[32,2048]{1,0:T(8,128)(2,1)} %q_ref.1, bf16[256,7680]{1,0:T(8,128)(2,1)} %vision_ref.1, bf16[960,256]{1,0:T(8,128)(2,1)} %key_ref.1, bf16[960,256]{1,0:T(8,128)(2,1)} %value_ref.1, bf16[2048,1024]{1,0:T(8,128)(2,1)} %out_w_ref.1, bf16[128,1024]{1,0:T(8,128)(2,1)} %res_ref.1, ...), custom_call_target="tpu_custom_call" | custom-call | tf_op jit(solution)/shard_map/pallas_call | solution.py:483
  95.8 1.7 %copy.12 = bf16[128,1024]{1,0:T(8,128)(2,1)} copy(bf16[128,1024]{1,0:T(8,128)(2,1)} %shard_map.91) | data formatting | bytes 524288
